TPU v7x, 512 devices: a whole 4x8x8 slice. The times are simulated.
512 devices in a mesh: dp: 32 (over y_lo, x, core), shard: 16 (over y_hi, z).
Axes of the slice: x: 4, y: 8 (y_hi: 2, y_lo: 4; y = y_hi * 4 + y_lo), z: 8, core: 2. Of those that a mesh axis runs over, the one named last changes fastest.
Arguments:
- tokens: bfloat16 [32768, 8192], P('dp', 'shard'), may hold values from -6 to 6
- weight_t: bfloat16 [1024, 8192], P('dp', 'shard'), may hold values from -0.0625 to 0.0625
- cotangent: bfloat16 [32768, 1024], P('dp'), may hold values from -6 to 6
- hard_ids: int32 [32, 8], P('dp'), may hold values from 0 to 7, each once within a row
- hard_count: int32 [32], replicated, may hold values from 0 to 8, as said below
Outputs:
- kv_rows: bfloat16 [32768, 1024], P(('dp', 'shard'))
- token_grad: bfloat16 [32768, 8192], P('dp', 'shard')
- weight_grad: float32 [1024, 8192], P('dp', 'shard')
Inputs may be any that keep to these rules, and one draw needn't show every extreme that they name: `hard_count`: the counts sum to 128; in every draw one group has 8 hard sequences and another none.
All inputs are finite; a program needn't handle non-finite values.
Results may differ from a plain program's by a relative error of at most 0.022.
Values may be sent and summed in bfloat16 or wider, within the bound.
A program may use at most 64 MiB of HBM per device.

v0:
```python
import math

import jax
import jax.numpy as jnp
from jax import lax
from jax.sharding import Mesh
from jax.sharding import PartitionSpec as P

SEQS = 8
L = 128
HARD_DEV = 4
SHARD = ("shard_0", "shard_1")
DP_SHARD = ("dp", "shard_0", "shard_1")


def in_blocks(x, dim, devices):
    before, after = (x.shape[:dim], x.shape[dim + 1 :])
    return jnp.moveaxis(x.reshape(*before, devices, -1, *after), dim, 0)


def sent_and_summed(x, axis, dim):
    blocks = in_blocks(x, dim, lax.axis_size(axis))
    arrived = lax.all_to_all(blocks, axis, split_axis=0, concat_axis=0, tiled=True)
    return arrived.astype(jnp.float32).sum(axis=0)


def in_order(blocks, dim):
    blocks = jnp.moveaxis(blocks, 0, dim)
    shape = blocks.shape
    return blocks.reshape(*shape[:dim], shape[dim] * shape[dim + 1], *shape[dim + 2 :])


def from_everyone(x, axis):
    devices = lax.axis_size(axis)
    return lax.all_to_all(jnp.broadcast_to(x[None], (devices, *x.shape)), axis, 0, 0, tiled=True)


def collect(x, axis, dim):
    return in_order(from_everyone(x, axis), dim)


def own_block(blocks, axes, turns):
    inside = blocks.shape[1:]
    blocks = blocks.reshape(*(lax.axis_size(a) for a in axes), *inside)
    blocks = jnp.moveaxis(blocks, turns, range(len(axes))).reshape(-1, *inside)
    for k in turns:
        blocks = lax.psum_scatter(blocks, axes[k], scatter_dimension=0, tiled=True)
    return blocks[0]


def summed_rows(x, axes, turns, dim):
    devices = lax.axis_size(axes)
    return own_block(in_blocks(x, dim, devices), axes, turns)


def grad_total(grad_rows, input_rows, factor):
    product = lax.dot_general(
        grad_rows, input_rows, (((0,), (0,)), ((), ())), preferred_element_type=jnp.float32
    )
    return sent_and_summed((product * factor).astype(jnp.bfloat16), "dp", 0)


def per_device(tokens, weight_t, cotangent, hard_ids, hard_count):
    groups = lax.axis_size("dp")
    group_index = lax.axis_index("dp")
    rows = tokens.shape[0]
    width_dev = tokens.shape[1]
    gathered = collect(weight_t, "dp", 0)
    kv_rows = (
        summed_rows(
            lax.dot_general(
                tokens, gathered, (((1,), (1,)), ((), ())), preferred_element_type=jnp.float32
            ).astype(jnp.bfloat16),
            SHARD,
            (1, 0),
            0,
        )
        .astype(jnp.float32)
        .astype(jnp.bfloat16)
    )
    backward_weight = collect(weight_t, "dp", 0)
    own_count = hard_count[group_index]
    order = hard_ids[0]
    picked = jnp.take(tokens.reshape(SEQS, L, width_dev), order, axis=0).reshape(rows, width_dev)
    slot_live = jnp.arange(SEQS, dtype=jnp.int32) < own_count
    row_live = jnp.repeat(slot_live, L)[:, None]
    picked = jnp.where(row_live, picked, jnp.zeros_like(picked))
    grads = jnp.where(row_live, cotangent, jnp.zeros_like(cotangent))
    factor = 1.0 / math.sqrt(groups * HARD_DEV * L)
    token_grad = jnp.dot(grads, backward_weight, preferred_element_type=jnp.float32).astype(
        jnp.bfloat16
    )
    weight_grad = grad_total(grads, picked, factor)
    return (kv_rows, token_grad, weight_grad)


def solution(mesh):
    finer = Mesh(mesh.devices.reshape(mesh.shape["dp"], 2, 8), ("dp", "shard_0", "shard_1"))
    return jax.shard_map(
        per_device,
        mesh=finer,
        in_specs=(P("dp", SHARD), P("dp", SHARD), P("dp", None), P("dp", None), P()),
        out_specs=(P(DP_SHARD, None), P("dp", SHARD), P("dp", SHARD)),
        check_vma=False,
    )
```

profile of v0, /device:TPU:1, one launch (start us, length us, event | category | flops | bytes accessed | tf_op | source)
XLA Modules:
  0.0 127.9 jit_solution(14247149005524989007)
XLA Ops:
  7.2 0.0 copy-start
  7.2 0.0 reduce-scatter.3.cloned.1.call-start
  7.2 0.9 broadcast_in_dim.51
  8.2 36.2 %all_to_all.11 = bf16[32,32,512]{2,1,0:T(8,128)(2,1)S(1)} all-to-all(bf16[32,32,512]{2,1,0:T(8,128)(2,1)S(1)} %broadcast_in_dim.51), channel_id=1, replica_groups=mesh['dp'=32,'shard_0'=2,'shard_1'=8] {'dp'}, dimensions={0} | all-to-all | bytes 2097152 | tf_op jit(solution)/shard_map/all_to_all | solution.py:35
  44.4 0.0 copy-done
  44.4 1.3 %convolution_convert_fusion = bf16[1024,1024]{1,0:T(8,128)(2,1)S(1)} fusion(bf16[1024,512]{1,0:T(8,128)(2,1)S(1)} %copy-done, bf16[1024,512]{1,0:T(8,128)(2,1)S(1)} %bitcast.30), kind=kOutput, calls=%fused_computation.4 | convolution fusion | flops 1074790400 | bytes 4194304 | tf_op jit(solution)/shard_map/dot_general | solution.py:71
  45.7 1.5 %copy.8 = bf16[8,2,64,1024]{3,2,1,0:T(8,128)(2,1)} copy(bf16[8,2,64,1024]{3,2,0,1:T(8,128)(2,1)S(1)} %bitcast.29) | data formatting | bytes 4194304 | tf_op jit(solution)/shard_map/transpose | solution.py:45
  47.2 0.0 copy-start.2
  47.2 0.0 copy-start.3
  47.2 0.0 reduce-scatter.3.cloned.1.call-update
  47.2 0.6 copy-done.2
  47.9 0.6 dynamic_slice.3
  48.5 0.0 copy-done.3
  48.5 0.6 gather_fusion
  49.1 0.0 copy-start.1
  49.1 0.8 iota_compare_fusion
  49.9 0.1 broadcast_bitcast_fusion.1
  50.0 0.1 broadcast_bitcast_fusion
  50.1 0.9 fusion
  51.0 0.0 copy-done.1
  51.0 2.4 %multiply_convert_fusion = bf16[1024,512]{1,0:T(8,128)(2,1)} fusion(bf16[1024,512]{1,0:T(8,128)(2,1)S(1)} %fusion, bf16[1024,1024]{1,0:T(8,128)(2,1)S(1)} %copy-done.1, pred[1024]{0:T(1024)(128)(4,1)S(1)} %broadcast_bitcast_fusion.1), kind=kOutput, calls=%fused_computation.2 | convolution fusion | flops 1075838976 | bytes 4195328 | tf_op jit(solution)/shard_map/dot_general | solution.py:57
  53.4 5.1 %all-to-all-start.1 = ((bf16[32,32,512]{2,1,0:T(8,128)(2,1)}), bf16[32,32,512]{2,1,0:T(8,128)(2,1)S(1)}, u32[]{:S(2)}, u32[]{:S(2)}) async-start(bf16[32,32,512]{2,1,0:T(8,128)(2,1)} %bitcast.32), calls=%async_computation.3 | async-start | bytes 2097152 | tf_op jit(solution)/shard_map/all_to_all | solution.py:23
  58.5 0.0 reduce-scatter.5.cloned.1.call-start
  58.6 30.6 %reduce-scatter.3.cloned.1.call-done = bf16[2,64,1024]{2,1,0:T(8,128)(2,1)} async-done(((bf16[16,64,1024]{2,1,0:T(8,128)(2,1)}), bf16[2,64,1024]{2,1,0:T(8,128)(2,1)}) %reduce-scatter.3.cloned.1.call-update) | async-done | bytes 262160 | tf_op jit(solution)/shard_map/reduce_scatter | solution.py:47
  89.2 0.0 reduce-scatter.5.cloned.1.call-update
  89.2 0.0 all-to-all-done.1
  89.2 0.8 convert_reduce_fusion
  90.0 3.9 %convolution_convert_fusion.1 = bf16[1024,512]{1,0:T(8,128)(2,1)} fusion(bf16[1024,512]{1,0:T(8,128)(2,1)S(1)} %bitcast.31, bf16[1024,1024]{1,0:T(8,128)(2,1)} %param.7, pred[1024]{0:T(1024)(128)(4,1)S(1)} %broadcast_bitcast_fusion.1), kind=kOutput, calls=%fused_computation.5 | convolution fusion | flops 1075314688 | bytes 4195328 | tf_op jit(solution)/shard_map/dot_general | solution.py:90
  93.9 27.2 %reduce-scatter.5.cloned.1.call-done = bf16[1,64,1024]{2,1,0:T(8,128)(2,1)} async-done(((bf16[2,64,1024]{2,1,0:T(8,128)(2,1)}), bf16[1,64,1024]{2,1,0:T(8,128)(2,1)}) %reduce-scatter.5.cloned.1.call-update) | async-done | bytes 131088 | tf_op jit(solution)/shard_map/reduce_scatter | solution.py:47
  (3 shorter events, 0.0 us)
Async XLA Ops:
  7.2 37.3 %copy-start = (bf16[1024,512]{1,0:T(8,128)(2,1)S(1)}, bf16[1024,512]{1,0:T(8,128)(2,1)}, u32[]{:S(2)}) copy-start(bf16[1024,512]{1,0:T(8,128)(2,1)} %param.5) | copy-start | bytes 3145732
  7.2 82.0 %reduce-scatter.3.cloned.1.call-start = ((), (), s32[]{:S(2)}) async-start(), calls=%async_computation.4 | async-start | bytes 2359296 | tf_op jit(solution)/shard_map/reduce_scatter | solution.py:47
  47.2 0.7 copy-start.2
  47.2 1.2 copy-start.3
  49.1 1.9 %copy-start.1 = (bf16[1024,1024]{1,0:T(8,128)(2,1)S(1)}, bf16[1024,1024]{1,0:T(8,128)(2,1)}, u32[]{:S(2)}) copy-start(bf16[1024,1024]{1,0:T(8,128)(2,1)} %param.7) | copy-start | bytes 6291460
  53.4 35.8 %all-to-all-start.1 = ((bf16[32,32,512]{2,1,0:T(8,128)(2,1)}), bf16[32,32,512]{2,1,0:T(8,128)(2,1)S(1)}, u32[]{:S(2)}, u32[]{:S(2)}) async-start(bf16[32,32,512]{2,1,0:T(8,128)(2,1)} %bitcast.32), calls=%async_computation.3 | async-start | bytes 2097152 | tf_op jit(solution)/shard_map/all_to_all | solution.py:23
  58.5 62.6 %reduce-scatter.5.cloned.1.call-start = ((), (), s32[]{:S(2)}) async-start(), calls=%async_computation.5 | async-start | bytes 393216 | tf_op jit(solution)/shard_map/reduce_scatter | solution.py:47
Sparse Core Ops, SparseCore 0:
  47.4 41.7 reduce-scatter.2
  92.5 28.5 reduce-scatter.4
where the time goes:
time: 128 us
  waiting for transfers between devices  57.9 us (45%)
  blocking collectives  36.2 us (28%)
  between operations  14.1 us (11%)
  matrix products  7.51 us (6%)
  starting transfers between devices  5.2 us (4%)
  local copies, waits for them, and re-layouts  4.43 us (3%)
  other arithmetic  2.51 us (2%)
    reduce_scatter x2, waiting for transfers between devices, own_block(): blocks = lax.psum_scatter(blocks, axes[k], scatter_dimension=0, tiled=True)  57.9 us
    all_to_all x1, blocking collectives, from_everyone(): lax.all_to_all(jnp.broadcast_to(x[None], (devices, *x.shape)), axis, 0, 0...  36.2 us
    all_to_all x1, starting transfers between devices, sent_and_summed(): lax.all_to_all(blocks, axis, split_axis=0, concat_axis=0, tiled=True)  5.12 us
    dot_general x1, matrix products, per_device(): jnp.dot(grads, backward_weight, preferred_element_type=jnp.float32)  3.85 us
  transfers between devices with their start and end apart: 3, of which 2 were waited for; matrix products, arithmetic and copies ran while one was open for 8% of the time, Pallas kernels for 0%

commit v1 on v0

v1 whole, which is shorter than its diff:
```python
import math

import jax
import jax.numpy as jnp
from jax import lax
from jax.experimental import pallas as pl
from jax.experimental.pallas import tpu as pltpu
from jax.sharding import PartitionSpec as P

SEQS = 8
L = 128
HARD_DEV = 4
CHUNKS = 4
NT = (((1,), (1,)), ((), ()))
TN = (((0,), (0,)), ((), ()))
F32 = jnp.float32
BF16 = jnp.bfloat16


def send(src, dst, send_sem, recv_sem, device):
    copy = pltpu.make_async_remote_copy(
        src_ref=src,
        dst_ref=dst,
        send_sem=send_sem,
        recv_sem=recv_sem,
        device_id=device,
        device_id_type=pl.DeviceIdType.MESH,
    )
    copy.start()
    return copy


def kernel(
    factor,
    ids,
    count,
    tok_hbm,
    w_hbm,
    cot_hbm,
    kv_out,
    tg_hbm,
    wg_out,
    tok,
    cot,
    w,
    pick,
    part,
    from_left,
    from_right,
    both,
    kept,
    from_half,
    grad,
    from_core,
    x1,
    x2r,
    x2l,
    ysum,
    from_y,
    tg,
    load_sem,
    tg_sem,
    w_send,
    w_recv,
    z_send,
    z_recv,
    h_send,
    h_recv,
    c_send,
    c_recv,
    x1_send,
    x1_recv,
    x2_send,
    x2_recv,
    y_send,
    y_recv,
):
    d = lax.axis_index("dp")
    s = lax.axis_index("shard")
    c = d % 2
    x = (d // 2) % 4
    y = d // 8
    z = s % 8
    half = s // 8
    xr, xl, xo = (x + 1) % 4, (x + 3) % 4, (x + 2) % 4
    right = (d, half * 8 + (z + 1) % 8)
    left = (d, half * 8 + (z + 7) % 8)
    other_half = (d, (1 - half) * 8 + z)

    def at(yy, xx, cc):
        return (yy * 4 + xx) * 2 + cc

    core = (at(y, x, 1 - c), s)
    x_right = (at(y, xr, c), s)
    x_left = (at(y, xl, c), s)
    ys = [(y + k) % 4 for k in range(4)]
    y_peers = [(at(ys[k], x, c), s) for k in range(1, 4)]

    barrier = pltpu.get_barrier_semaphore()
    peers = [*y_peers, x_right, x_left, core, right, left, other_half]
    for peer in peers:
        pl.semaphore_signal(barrier, inc=1, device_id=peer, device_id_type=pl.DeviceIdType.MESH)

    def block(index):
        return w.at[pl.ds(pl.multiple_of(index * 32, 32), 32), :]

    loads = [
        pltpu.make_async_copy(w_hbm, block(d), load_sem.at[0]),
        pltpu.make_async_copy(tok_hbm, tok, load_sem.at[1]),
        pltpu.make_async_copy(cot_hbm, cot, load_sem.at[2]),
    ]
    for load in loads:
        load.start()
    loads[0].wait()
    pl.semaphore_wait(barrier, len(peers))

    sent = []

    def w_to(index, device):
        sent.append(send(block(index), block(index), w_send.at[len(sent)], w_recv.at[index], device))

    def w_wait(index):
        pltpu.make_async_remote_copy(
            src_ref=block(index),
            dst_ref=block(index),
            send_sem=w_send.at[0],
            recv_sem=w_recv.at[index],
            device_id=core,
            device_id_type=pl.DeviceIdType.MESH,
        ).wait_recv()

    for peer in reversed(y_peers):
        w_to(d, peer)
    for peer in (x_right, x_left, core):
        w_to(d, peer)

    own_count = count[d]

    def live(k):
        return jnp.clip(own_count - k, 0, 1).astype(F32)

    loads[1].wait()
    for k in range(SEQS):
        rows = tok[ids[0, k]].astype(F32) * live(k)
        pick[k * L : (k + 1) * L, :] = rows.astype(BF16)
    loads[2].wait()

    c_copies = []

    def grad_piece(j):
        product = lax.dot_general(
            cot[:, j * 256 : (j + 1) * 256], pick[...], TN, preferred_element_type=F32
        )
        product = (product * factor).astype(BF16).reshape(4, 2, 32, 512)
        for cc in range(2):
            grad[cc, j] = product[:, cc]
        c_copies.append(
            send(grad.at[1 - c, j], from_core.at[j], c_send.at[j], c_recv.at[j], core)
        )

    grad_piece(0)
    for k in range(1, 4):
        w_wait(at(ys[k], x, c))
        for peer in (x_right, x_left, core):
            w_to(at(ys[k], x, c), peer)
    grad_piece(1)
    for k in range(4):
        from_l, from_r = at(ys[k], xl, c), at(ys[k], xr, c)
        w_wait(from_l)
        if k < 2:
            w_to(from_l, x_right)
        w_to(from_l, core)
        w_wait(from_r)
        if k >= 2:
            w_to(from_r, x_left)
        w_to(from_r, core)
    for k in range(4):
        w_wait(at(ys[k], xo, c))
        w_to(at(ys[k], xo, c), core)
    for yy in range(4):
        for xx in range(4):
            w_wait(at(yy, xx, 1 - c))

    width = 1024 // CHUNKS
    z_copies = {}
    h_copies = []

    def z_right(j, r, src, dst):
        z_copies[0, j, r] = send(src, dst, z_send.at[0, j, r], z_recv.at[0, j, r], right)

    def z_left(j, r, src, dst):
        z_copies[1, j, r] = send(src, dst, z_send.at[1, j, r], z_recv.at[1, j, r], left)

    def start_chunk(j):
        for h in range(2):
            product = lax.dot_general(
                tok[h * 4 : (h + 1) * 4].reshape(512, 512),
                w[j * width : (j + 1) * width, :],
                NT,
                preferred_element_type=F32,
            )
            part[j, :, h] = product.astype(BF16).reshape(8, 64, width)
        far = (z + 4) % 8
        z_right(j, 0, part.at[j, far, 0], from_left.at[j, 0, 0])
        z_left(j, 0, part.at[j, far, 1], from_right.at[j, 0, 1])

    def add_into(ref, index, other):
        ref[index] = (ref[index].astype(F32) + other.astype(F32)).astype(BF16)

    def z_round(j, r):
        to_right, to_left = (z + 4 - r) % 8, (z + 4 + r) % 8
        z_copies[0, j, r - 1].wait_recv()
        if r == 1:
            add_into(part, (j, to_right, 0), from_left[j, 0, 0])
        else:
            add_into(part, (j, to_right), from_left[j, r - 1])
        z_right(j, r, part.at[j, to_right], from_left.at[j, r])
        z_copies[1, j, r - 1].wait_recv()
        if r == 1:
            add_into(part, (j, to_left, 1), from_right[j, 0, 1])
        else:
            add_into(part, (j, to_left), from_right[j, r - 1])
        z_left(j, r, part.at[j, to_left], from_right.at[j, r])

    def z_finish(j):
        z_copies[0, j, 3].wait_recv()
        z_copies[1, j, 3].wait_recv()
        total = part[j, z].astype(F32) + from_left[j, 3].astype(F32) + from_right[j, 3].astype(F32)
        kept[j] = total
        both[j] = total.astype(BF16)
        h_copies.append(
            send(both.at[j, 1 - half], from_half.at[j], h_send.at[j], h_recv.at[j], other_half)
        )

    def kv_finish(j):
        h_copies[j].wait_recv()
        total = kept[j, half] + from_half[j].astype(F32)
        kv_out[:, j * width : (j + 1) * width] = total.astype(BF16)

    x1_copies = {}
    x2_copies = {}
    y_copies = []

    def grad_core():
        for j in range(4):
            c_copies[j].wait_recv()
            add_into(grad, (c, j), from_core[j])
        for j in range(4):
            x1_copies[j] = send(
                grad.at[c, j, xo],
                x1.at[j],
                x1_send.at[j],
                x1_recv.at[j],
                x_right if j < 2 else x_left,
            )
        for j in (2, 3):
            x2_copies[0, j] = send(
                grad.at[c, j, xr], x2r.at[j], x2_send.at[0, j], x2_recv.at[0, j], x_right
            )
        for j in (0, 1):
            x2_copies[1, j] = send(
                grad.at[c, j, xl], x2l.at[j], x2_send.at[1, j], x2_recv.at[1, j], x_left
            )

    def grad_x():
        for j in range(2):
            x1_copies[j].wait_recv()
            add_into(grad, (c, j, xr), x1[j])
            x2_copies[0, j] = send(
                grad.at[c, j, xr], x2r.at[j], x2_send.at[0, j], x2_recv.at[0, j], x_right
            )
        for j in range(2, 4):
            x1_copies[j].wait_recv()
            add_into(grad, (c, j, xl), x1[j])
            x2_copies[1, j] = send(
                grad.at[c, j, xl], x2l.at[j], x2_send.at[1, j], x2_recv.at[1, j], x_left
            )

    def grad_y():
        for j in range(4):
            x2_copies[0, j].wait_recv()
            x2_copies[1, j].wait_recv()
        for j in range(4):
            total = grad[c, j, x].astype(F32) + x2r[j].astype(F32) + x2l[j].astype(F32)
            ysum[j] = total.astype(BF16)
        for k in range(1, 4):
            y_copies.append(
                send(
                    ysum.at[ys[k]],
                    from_y.at[k - 1],
                    y_send.at[k - 1],
                    y_recv.at[k - 1],
                    y_peers[k - 1],
                )
            )

    def grad_finish():
        total = ysum[y].astype(F32)
        for k in range(3):
            y_copies[k].wait_recv()
            total = total + from_y[k].astype(F32)
        wg_out[...] = total

    tg_copies = []

    def token_piece(p):
        rows = slice(p * 256, (p + 1) * 256)
        product = jnp.dot(cot[rows, :], w[...], preferred_element_type=F32)
        for i in range(2):
            own = product[i * L : (i + 1) * L] * live(2 * p + i)
            tg[p * 256 + i * L : p * 256 + (i + 1) * L, :] = own.astype(BF16)
        copy = pltpu.make_async_copy(tg.at[rows, :], tg_hbm.at[rows, :], tg_sem.at[p])
        copy.start()
        tg_copies.append(copy)

    beside = {
        0: [lambda: grad_piece(2)],
        1: [lambda: grad_piece(3), grad_core],
        2: [grad_x, lambda: token_piece(0)],
        3: [grad_y, lambda: token_piece(1)],
        4: [grad_finish, lambda: token_piece(2)],
        5: [lambda: token_piece(3)],
    }
    for t in range(CHUNKS + 6):
        if t < CHUNKS:
            start_chunk(t)
        for r in (4, 3, 2, 1):
            j = t - r
            if 0 <= j < CHUNKS:
                if r == 4:
                    z_finish(j)
                else:
                    z_round(j, r)
        for extra in beside.get(t, []):
            extra()
        if 0 <= t - 6 < CHUNKS:
            kv_finish(t - 6)

    everything = [*sent, *c_copies, *z_copies.values(), *h_copies]
    everything += [*x1_copies.values(), *x2_copies.values(), *y_copies]
    for copy in everything:
        copy.wait_send()
    for copy in tg_copies:
        copy.wait()


def per_device(tokens, weight_t, cotangent, hard_ids, hard_count):
    factor = 1.0 / math.sqrt(lax.axis_size("dp") * HARD_DEV * L)
    rows, width = tokens.shape
    chans = cotangent.shape[1]
    wide = chans // CHUNKS
    any_spec = pl.BlockSpec(memory_space=pl.ANY)
    smem = pl.BlockSpec(memory_space=pltpu.SMEM)
    vmem = pl.BlockSpec(memory_space=pltpu.VMEM)
    dma = pltpu.SemaphoreType.DMA

    def body(*refs):
        kernel(factor, *refs)

    return pl.pallas_call(
        body,
        out_shape=(
            jax.ShapeDtypeStruct((64, chans), BF16),
            jax.ShapeDtypeStruct((rows, width), BF16),
            jax.ShapeDtypeStruct((32, width), F32),
        ),
        in_specs=[smem, smem, any_spec, any_spec, any_spec],
        out_specs=(vmem, any_spec, vmem),
        scratch_shapes=[
            pltpu.VMEM((SEQS, L, width), BF16),
            pltpu.VMEM((rows, chans), BF16),
            pltpu.VMEM((chans, width), BF16),
            pltpu.VMEM((rows, width), BF16),
            pltpu.VMEM((CHUNKS, 8, 2, 64, wide), BF16),
            pltpu.VMEM((CHUNKS, 4, 2, 64, wide), BF16),
            pltpu.VMEM((CHUNKS, 4, 2, 64, wide), BF16),
            pltpu.VMEM((CHUNKS, 2, 64, wide), BF16),
            pltpu.VMEM((CHUNKS, 2, 64, wide), F32),
            pltpu.VMEM((CHUNKS, 64, wide), BF16),
            pltpu.VMEM((2, 4, 4, 32, width), BF16),
            pltpu.VMEM((4, 4, 32, width), BF16),
            pltpu.VMEM((4, 32, width), BF16),
            pltpu.VMEM((4, 32, width), BF16),
            pltpu.VMEM((4, 32, width), BF16),
            pltpu.VMEM((4, 32, width), BF16),
            pltpu.VMEM((3, 32, width), BF16),
            pltpu.VMEM((rows, width), BF16),
            dma((3,)),
            dma((4,)),
            dma((40,)),
            dma((32,)),
            dma((2, CHUNKS, 4)),
            dma((2, CHUNKS, 4)),
            dma((CHUNKS,)),
            dma((CHUNKS,)),
            dma((4,)),
            dma((4,)),
            dma((4,)),
            dma((4,)),
            dma((2, 4)),
            dma((2, 4)),
            dma((3,)),
            dma((3,)),
        ],
        compiler_params=pltpu.CompilerParams(collective_id=0, has_side_effects=True),
    )(hard_ids, hard_count, tokens.reshape(SEQS, L, width), weight_t, cotangent)


def solution(mesh):
    return jax.shard_map(
        per_device,
        mesh=mesh,
        in_specs=(P("dp", "shard"), P("dp", "shard"), P("dp", None), P("dp", None), P()),
        out_specs=(P(("dp", "shard"), None), P("dp", "shard"), P("dp", "shard")),
        check_vma=False,
    )
```

time: 128 us -> 68.7 us (0.54)
  the two profiles are of different devices: /device:TPU:1 before, /device:TPU:56 now
where the time goes in v1:
time: 68.7 us; the launch traced here: 68.5 us
  Pallas kernels  63.3 us (92%)
  local copies, waits for them, and re-layouts  4.49 us (7%)
    pallas_call x1, Pallas kernels, per_device(): pl.pallas_call(body, out_shape=(jax.ShapeDtypeStruct((64, chans), BF16),...  63.3 us
    unnamed x5, local copies, waits for them, and re-layouts  4.49 us

profile of v1, /device:TPU:56, one launch (start us, length us, event | category | flops | bytes accessed | tf_op | source)
XLA Modules:
  0.0 68.5 jit_solution(9866622199332395129)
XLA Ops:
  0.6 63.3 %shard_map.76 = (bf16[64,1024]{1,0:T(8,128)(2,1)}, bf16[1024,512]{1,0:T(8,128)(2,1)}, f32[32,512]{1,0:T(8,128)}) custom-call(s32[1,8]{1,0:T(1,128)} %refs_0_.1, s32[32]{0:T(128)} %refs_1_.1, bf16[8,128,512]{2,1,0:T(8,128)(2,1)} %bitcast.1, bf16[32,512]{1,0:T(8,128)(2,1)} %refs_3_.1, bf16[1024,1024]{1,0:T(8,128)(2,1)} %refs_4_.1), custom_call_target="tpu_custom_call" | custom-call | tf_op jit(solution)/shard_map/pallas_call | solution.py:360
  64.0 0.0 copy-start
  64.0 1.6 %copy.11 = bf16[64,1024]{1,0:T(8,128)(2,1)} copy(bf16[64,1024]{1,0:T(8,128)(2,1)} %get-tuple-element.6) | data formatting | bytes 262144
  65.6 2.3 %copy.12 = bf16[1024,512]{1,0:T(8,128)(2,1)} copy(bf16[1024,512]{1,0:T(8,128)(2,1)} %get-tuple-element.7) | data formatting | bytes 2097152
  67.9 0.0 copy-done
  67.9 0.6 copy.13
Async XLA Ops:
  64.0 3.9 %copy-start = (f32[32,512]{1,0:T(8,128)S(1)}, f32[32,512]{1,0:T(8,128)}, u32[]{:S(2)}) copy-start(f32[32,512]{1,0:T(8,128)} %get-tuple-element.8) | copy-start | bytes 196612

commit v2 on v1

--- a/solution.py
+++ b/solution.py
@@ -61,6 +61,7 @@
     load_sem,
     tg_sem,
     w_send,
+    f_send,
     w_recv,
     z_send,
     z_recv,
@@ -116,23 +117,29 @@
 
     sent = []
 
-    def w_to(index, device):
-        sent.append(send(block(index), block(index), w_send.at[len(sent)], w_recv.at[index], device))
-
-    def w_wait(index):
-        pltpu.make_async_remote_copy(
+    def w_copy(index, send_sem, device):
+        return pltpu.make_async_remote_copy(
             src_ref=block(index),
             dst_ref=block(index),
-            send_sem=w_send.at[0],
+            send_sem=send_sem,
             recv_sem=w_recv.at[index],
-            device_id=core,
+            device_id=device,
             device_id_type=pl.DeviceIdType.MESH,
-        ).wait_recv()
-
-    for peer in reversed(y_peers):
+        )
+
+    def w_to(index, device):
+        copy = w_copy(index, w_send.at[len(sent)], device)
+        copy.start()
+        sent.append(copy)
+
+    def w_wait(index):
+        w_copy(index, w_send.at[0], core).wait_recv()
+
+    beside_x = (x_right, x_left, core)
+    for peer in y_peers:
         w_to(d, peer)
-    for peer in (x_right, x_left, core):
-        w_to(d, peer)
+    for p, peer in enumerate(beside_x):
+        w_copy(d, f_send.at[y, p], peer).start()
 
     own_count = count[d]
 
@@ -158,28 +165,38 @@
             send(grad.at[1 - c, j], from_core.at[j], c_send.at[j], c_recv.at[j], core)
         )
 
-    grad_piece(0)
-    for k in range(1, 4):
-        w_wait(at(ys[k], x, c))
-        for peer in (x_right, x_left, core):
-            w_to(at(ys[k], x, c), peer)
-    grad_piece(1)
-    for k in range(4):
-        from_l, from_r = at(ys[k], xl, c), at(ys[k], xr, c)
+    def along_x(j):
+        @pl.when(j != y)
+        def _():
+            w_wait(at(j, x, c))
+            for p, peer in enumerate(beside_x):
+                w_copy(at(j, x, c), f_send.at[j, p], peer).start()
+
+    def around_x(j):
+        from_l, from_r = at(j, xl, c), at(j, xr, c)
         w_wait(from_l)
-        if k < 2:
+        if j % 2 == 0:
             w_to(from_l, x_right)
         w_to(from_l, core)
         w_wait(from_r)
-        if k >= 2:
+        if j % 2 == 1:
             w_to(from_r, x_left)
         w_to(from_r, core)
-    for k in range(4):
-        w_wait(at(ys[k], xo, c))
-        w_to(at(ys[k], xo, c), core)
-    for yy in range(4):
+
+    def across_x(j):
+        w_wait(at(j, xo, c))
+        w_to(at(j, xo, c), core)
+
+    def chunk_here(j):
         for xx in range(4):
-            w_wait(at(yy, xx, 1 - c))
+            w_wait(at(j, xx, 1 - c))
+
+    grad_piece(0)
+    for j in range(4):
+        along_x(j)
+    grad_piece(1)
+    for j in range(4):
+        around_x(j)
 
     width = 1024 // CHUNKS
     z_copies = {}
@@ -200,26 +217,35 @@
                 preferred_element_type=F32,
             )
             part[j, :, h] = product.astype(BF16).reshape(8, 64, width)
-        far = (z + 4) % 8
+        far, near_r, near_l = (z + 4) % 8, (z + 3) % 8, (z + 5) % 8
         z_right(j, 0, part.at[j, far, 0], from_left.at[j, 0, 0])
         z_left(j, 0, part.at[j, far, 1], from_right.at[j, 0, 1])
+        z_right(j, 4, part.at[j, near_r, 1], from_left.at[j, 1, 1])
+        z_left(j, 4, part.at[j, near_l, 0], from_right.at[j, 1, 0])
 
     def add_into(ref, index, other):
         ref[index] = (ref[index].astype(F32) + other.astype(F32)).astype(BF16)
+
+    def z_first(j):
+        to_right, to_left = (z + 3) % 8, (z + 5) % 8
+        z_copies[0, j, 0].wait_recv()
+        add_into(part, (j, to_right, 0), from_left[j, 0, 0])
+        z_right(j, 1, part.at[j, to_right, 0], from_left.at[j, 1, 0])
+        z_copies[1, j, 0].wait_recv()
+        add_into(part, (j, to_left, 1), from_right[j, 0, 1])
+        z_left(j, 1, part.at[j, to_left, 1], from_right.at[j, 1, 1])
 
     def z_round(j, r):
         to_right, to_left = (z + 4 - r) % 8, (z + 4 + r) % 8
         z_copies[0, j, r - 1].wait_recv()
-        if r == 1:
-            add_into(part, (j, to_right, 0), from_left[j, 0, 0])
-        else:
-            add_into(part, (j, to_right), from_left[j, r - 1])
+        if r == 2:
+            z_copies[0, j, 4].wait_recv()
+        add_into(part, (j, to_right), from_left[j, r - 1])
         z_right(j, r, part.at[j, to_right], from_left.at[j, r])
         z_copies[1, j, r - 1].wait_recv()
-        if r == 1:
-            add_into(part, (j, to_left, 1), from_right[j, 0, 1])
-        else:
-            add_into(part, (j, to_left), from_right[j, r - 1])
+        if r == 2:
+            z_copies[1, j, 4].wait_recv()
+        add_into(part, (j, to_left), from_right[j, r - 1])
         z_left(j, r, part.at[j, to_left], from_right.at[j, r])
 
     def z_finish(j):
@@ -313,29 +339,43 @@
         copy.start()
         tg_copies.append(copy)
 
-    beside = {
-        0: [lambda: grad_piece(2)],
-        1: [lambda: grad_piece(3), grad_core],
-        2: [grad_x, lambda: token_piece(0)],
-        3: [grad_y, lambda: token_piece(1)],
-        4: [grad_finish, lambda: token_piece(2)],
-        5: [lambda: token_piece(3)],
-    }
-    for t in range(CHUNKS + 6):
-        if t < CHUNKS:
-            start_chunk(t)
-        for r in (4, 3, 2, 1):
-            j = t - r
-            if 0 <= j < CHUNKS:
-                if r == 4:
-                    z_finish(j)
-                else:
-                    z_round(j, r)
-        for extra in beside.get(t, []):
-            extra()
-        if 0 <= t - 6 < CHUNKS:
-            kv_finish(t - 6)
-
+    across_x(0)
+    across_x(1)
+    for j in range(CHUNKS):
+        chunk_here(j)
+        start_chunk(j)
+        if j + 2 < CHUNKS:
+            across_x(j + 2)
+    for j in range(CHUNKS):
+        z_first(j)
+    grad_piece(2)
+    grad_piece(3)
+    z_round(0, 2)
+    z_round(1, 2)
+    grad_core()
+    z_round(2, 2)
+    z_round(3, 2)
+    token_piece(0)
+    z_round(0, 3)
+    grad_x()
+    z_round(1, 3)
+    token_piece(1)
+    z_round(2, 3)
+    grad_y()
+    z_round(3, 3)
+    z_finish(0)
+    token_piece(2)
+    z_finish(1)
+    token_piece(3)
+    z_finish(2)
+    grad_finish()
+    z_finish(3)
+    for j in range(CHUNKS):
+        kv_finish(j)
+
+    for j in range(4):
+        for p in range(3):
+            w_copy(d, f_send.at[j, p], core).wait_send()
     everything = [*sent, *c_copies, *z_copies.values(), *h_copies]
     everything += [*x1_copies.values(), *x2_copies.values(), *y_copies]
     for copy in everything:
@@ -387,10 +427,11 @@
             pltpu.VMEM((rows, width), BF16),
             dma((3,)),
             dma((4,)),
-            dma((40,)),
+            dma((19,)),
+            dma((4, 3)),
             dma((32,)),
-            dma((2, CHUNKS, 4)),
-            dma((2, CHUNKS, 4)),
+            dma((2, CHUNKS, 5)),
+            dma((2, CHUNKS, 5)),
             dma((CHUNKS,)),
             dma((CHUNKS,)),
             dma((4,)),

time: 68.7 us -> 63.2 us (0.920)
  Pallas kernels: 63.3 us -> 57.4 us
    pallas_call x1, Pallas kernels: 63.3 us -> 57.4 us  [per_device(): pl.pallas_call(body, out_shape=(jax.ShapeDtypeStruct((64, chans), BF16),...]
where the time goes in v2:
time: 63.2 us; the launch traced here: 62.5 us
  Pallas kernels  57.4 us (91%)
  local copies, waits for them, and re-layouts  4.49 us (7%)
  between operations  0.65 us (1%)
    pallas_call x1, Pallas kernels, per_device(): pl.pallas_call(body, out_shape=(jax.ShapeDtypeStruct((64, chans), BF16),...  57.4 us
    unnamed x5, local copies, waits for them, and re-layouts  4.49 us

profile of v2, /device:TPU:56, one launch (start us, length us, event | category | flops | bytes accessed | tf_op | source)
XLA Modules:
  0.0 62.5 jit_solution(13133296812854176975)
XLA Ops:
  0.6 57.4 %shard_map.76 = (bf16[64,1024]{1,0:T(8,128)(2,1)}, bf16[1024,512]{1,0:T(8,128)(2,1)}, f32[32,512]{1,0:T(8,128)}) custom-call(s32[1,8]{1,0:T(1,128)} %refs_0_.1, s32[32]{0:T(128)} %refs_1_.1, bf16[8,128,512]{2,1,0:T(8,128)(2,1)} %bitcast.1, bf16[32,512]{1,0:T(8,128)(2,1)} %refs_3_.1, bf16[1024,1024]{1,0:T(8,128)(2,1)} %refs_4_.1), custom_call_target="tpu_custom_call" | custom-call | tf_op jit(solution)/shard_map/pallas_call | solution.py:400
  58.0 0.0 copy-start
  58.0 1.6 %copy.11 = bf16[64,1024]{1,0:T(8,128)(2,1)} copy(bf16[64,1024]{1,0:T(8,128)(2,1)} %get-tuple-element.6) | data formatting | bytes 262144
  59.6 2.3 %copy.12 = bf16[1024,512]{1,0:T(8,128)(2,1)} copy(bf16[1024,512]{1,0:T(8,128)(2,1)} %get-tuple-element.7) | data formatting | bytes 2097152
  61.9 0.0 copy-done
  61.9 0.6 %copy.13 = f32[32,512]{1,0:T(8,128)} copy(f32[32,512]{1,0:T(8,128)S(1)} %copy-done) | data formatting | bytes 131072
Async XLA Ops:
  58.0 3.9 %copy-start = (f32[32,512]{1,0:T(8,128)S(1)}, f32[32,512]{1,0:T(8,128)}, u32[]{:S(2)}) copy-start(f32[32,512]{1,0:T(8,128)} %get-tuple-element.8) | copy-start | bytes 196612

commit v3 on v2

--- a/solution.py
+++ b/solution.py
@@ -32,14 +32,16 @@
 
 def kernel(
     factor,
-    ids,
-    count,
+    ids_hbm,
+    count_hbm,
     tok_hbm,
     w_hbm,
     cot_hbm,
     kv_out,
-    tg_hbm,
+    tg,
     wg_out,
+    ids,
+    count,
     tok,
     cot,
     w,
@@ -48,7 +50,6 @@
     from_left,
     from_right,
     both,
-    kept,
     from_half,
     grad,
     from_core,
@@ -57,9 +58,7 @@
     x2l,
     ysum,
     from_y,
-    tg,
     load_sem,
-    tg_sem,
     w_send,
     f_send,
     w_recv,
@@ -109,6 +108,8 @@
         pltpu.make_async_copy(w_hbm, block(d), load_sem.at[0]),
         pltpu.make_async_copy(tok_hbm, tok, load_sem.at[1]),
         pltpu.make_async_copy(cot_hbm, cot, load_sem.at[2]),
+        pltpu.make_async_copy(ids_hbm, ids, load_sem.at[3]),
+        pltpu.make_async_copy(count_hbm, count, load_sem.at[4]),
     ]
     for load in loads:
         load.start()
@@ -141,6 +142,8 @@
     for p, peer in enumerate(beside_x):
         w_copy(d, f_send.at[y, p], peer).start()
 
+    loads[3].wait()
+    loads[4].wait()
     own_count = count[d]
 
     def live(k):
@@ -195,8 +198,12 @@
     for j in range(4):
         along_x(j)
     grad_piece(1)
-    for j in range(4):
-        around_x(j)
+    around_x(0)
+    around_x(1)
+    grad_piece(2)
+    around_x(2)
+    around_x(3)
+    grad_piece(3)
 
     width = 1024 // CHUNKS
     z_copies = {}
@@ -235,32 +242,47 @@
         add_into(part, (j, to_left, 1), from_right[j, 0, 1])
         z_left(j, 1, part.at[j, to_left, 1], from_right.at[j, 1, 1])
 
-    def z_round(j, r):
+    away = 1 - half
+
+    def z_step(j, r, h, last, this):
         to_right, to_left = (z + 4 - r) % 8, (z + 4 + r) % 8
-        z_copies[0, j, r - 1].wait_recv()
-        if r == 2:
-            z_copies[0, j, 4].wait_recv()
-        add_into(part, (j, to_right), from_left[j, r - 1])
-        z_right(j, r, part.at[j, to_right], from_left.at[j, r])
-        z_copies[1, j, r - 1].wait_recv()
-        if r == 2:
-            z_copies[1, j, 4].wait_recv()
-        add_into(part, (j, to_left), from_right[j, r - 1])
-        z_left(j, r, part.at[j, to_left], from_right.at[j, r])
-
-    def z_finish(j):
-        z_copies[0, j, 3].wait_recv()
-        z_copies[1, j, 3].wait_recv()
-        total = part[j, z].astype(F32) + from_left[j, 3].astype(F32) + from_right[j, 3].astype(F32)
-        kept[j] = total
-        both[j] = total.astype(BF16)
+        for index in last:
+            z_copies[0, j, index].wait_recv()
+        add_into(part, (j, to_right, h), from_left[j, r - 1, h])
+        z_right(j, this, part.at[j, to_right, h], from_left.at[j, r, h])
+        for index in last:
+            z_copies[1, j, index].wait_recv()
+        add_into(part, (j, to_left, h), from_right[j, r - 1, h])
+        z_left(j, this, part.at[j, to_left, h], from_right.at[j, r, h])
+
+    def second_away(j):
+        z_step(j, 2, away, (1, 4), 2)
+
+    def second_own(j):
+        z_step(j, 2, half, (), 5)
+
+    def third_away(j):
+        z_step(j, 3, away, (2,), 3)
+
+    def third_own(j):
+        z_step(j, 3, half, (5,), 6)
+
+    def z_total(j, h, index):
+        z_copies[0, j, index].wait_recv()
+        z_copies[1, j, index].wait_recv()
+        total = part[j, z, h].astype(F32) + from_left[j, 3, h].astype(F32)
+        return total + from_right[j, 3, h].astype(F32)
+
+    def to_other_half(j):
+        both[j] = z_total(j, away, 3).astype(BF16)
         h_copies.append(
-            send(both.at[j, 1 - half], from_half.at[j], h_send.at[j], h_recv.at[j], other_half)
+            send(both.at[j], from_half.at[j], h_send.at[j], h_recv.at[j], other_half)
         )
 
     def kv_finish(j):
+        total = z_total(j, half, 6)
         h_copies[j].wait_recv()
-        total = kept[j, half] + from_half[j].astype(F32)
+        total = total + from_half[j].astype(F32)
         kv_out[:, j * width : (j + 1) * width] = total.astype(BF16)
 
     x1_copies = {}
@@ -327,17 +349,12 @@
             total = total + from_y[k].astype(F32)
         wg_out[...] = total
 
-    tg_copies = []
-
     def token_piece(p):
         rows = slice(p * 256, (p + 1) * 256)
         product = jnp.dot(cot[rows, :], w[...], preferred_element_type=F32)
         for i in range(2):
             own = product[i * L : (i + 1) * L] * live(2 * p + i)
             tg[p * 256 + i * L : p * 256 + (i + 1) * L, :] = own.astype(BF16)
-        copy = pltpu.make_async_copy(tg.at[rows, :], tg_hbm.at[rows, :], tg_sem.at[p])
-        copy.start()
-        tg_copies.append(copy)
 
     across_x(0)
     across_x(1)
@@ -348,28 +365,30 @@
             across_x(j + 2)
     for j in range(CHUNKS):
         z_first(j)
-    grad_piece(2)
-    grad_piece(3)
-    z_round(0, 2)
-    z_round(1, 2)
     grad_core()
-    z_round(2, 2)
-    z_round(3, 2)
+    for j in range(CHUNKS):
+        second_away(j)
     token_piece(0)
-    z_round(0, 3)
     grad_x()
-    z_round(1, 3)
+    for j in range(CHUNKS):
+        second_own(j)
     token_piece(1)
-    z_round(2, 3)
+    third_away(0)
+    third_away(1)
     grad_y()
-    z_round(3, 3)
-    z_finish(0)
+    third_away(2)
+    third_away(3)
     token_piece(2)
-    z_finish(1)
+    third_own(0)
+    to_other_half(0)
+    third_own(1)
+    to_other_half(1)
+    third_own(2)
+    to_other_half(2)
+    third_own(3)
+    to_other_half(3)
     token_piece(3)
-    z_finish(2)
     grad_finish()
-    z_finish(3)
     for j in range(CHUNKS):
         kv_finish(j)
 
@@ -380,8 +399,6 @@
     everything += [*x1_copies.values(), *x2_copies.values(), *y_copies]
     for copy in everything:
         copy.wait_send()
-    for copy in tg_copies:
-        copy.wait()
 
 
 def per_device(tokens, weight_t, cotangent, hard_ids, hard_count):
@@ -390,7 +407,6 @@
     chans = cotangent.shape[1]
     wide = chans // CHUNKS
     any_spec = pl.BlockSpec(memory_space=pl.ANY)
-    smem = pl.BlockSpec(memory_space=pltpu.SMEM)
     vmem = pl.BlockSpec(memory_space=pltpu.VMEM)
     dma = pltpu.SemaphoreType.DMA
 
@@ -400,13 +416,15 @@
     return pl.pallas_call(
         body,
         out_shape=(
-            jax.ShapeDtypeStruct((64, chans), BF16),
-            jax.ShapeDtypeStruct((rows, width), BF16),
-            jax.ShapeDtypeStruct((32, width), F32),
+            pltpu.VMEM((64, chans), BF16),
+            pltpu.VMEM((rows, width), BF16),
+            pltpu.VMEM((32, width), F32),
         ),
-        in_specs=[smem, smem, any_spec, any_spec, any_spec],
-        out_specs=(vmem, any_spec, vmem),
+        in_specs=[any_spec] * 5,
+        out_specs=(vmem, vmem, vmem),
         scratch_shapes=[
+            pltpu.SMEM((1, SEQS), jnp.int32),
+            pltpu.SMEM(hard_count.shape, jnp.int32),
             pltpu.VMEM((SEQS, L, width), BF16),
             pltpu.VMEM((rows, chans), BF16),
             pltpu.VMEM((chans, width), BF16),
@@ -414,8 +432,7 @@
             pltpu.VMEM((CHUNKS, 8, 2, 64, wide), BF16),
             pltpu.VMEM((CHUNKS, 4, 2, 64, wide), BF16),
             pltpu.VMEM((CHUNKS, 4, 2, 64, wide), BF16),
-            pltpu.VMEM((CHUNKS, 2, 64, wide), BF16),
-            pltpu.VMEM((CHUNKS, 2, 64, wide), F32),
+            pltpu.VMEM((CHUNKS, 64, wide), BF16),
             pltpu.VMEM((CHUNKS, 64, wide), BF16),
             pltpu.VMEM((2, 4, 4, 32, width), BF16),
             pltpu.VMEM((4, 4, 32, width), BF16),
@@ -424,14 +441,12 @@
             pltpu.VMEM((4, 32, width), BF16),
             pltpu.VMEM((4, 32, width), BF16),
             pltpu.VMEM((3, 32, width), BF16),
-            pltpu.VMEM((rows, width), BF16),
-            dma((3,)),
-            dma((4,)),
+            dma((5,)),
             dma((19,)),
             dma((4, 3)),
             dma((32,)),
-            dma((2, CHUNKS, 5)),
-            dma((2, CHUNKS, 5)),
+            dma((2, CHUNKS, 7)),
+            dma((2, CHUNKS, 7)),
             dma((CHUNKS,)),
             dma((CHUNKS,)),
             dma((4,)),

time: 63.2 us -> 57.6 us (0.911)
  Pallas kernels: 57.4 us -> 54.6 us
  local copies, waits for them, and re-layouts: 4.49 us -> 2.26 us
    pallas_call x1, Pallas kernels: 57.4 us -> 54.6 us  [per_device(): pl.pallas_call(body, out_shape=(pltpu.VMEM((64, chans), BF16), pltpu.VMEM...]
    unnamed x5 -> x3, local copies, waits for them, and re-layouts: 4.49 us -> 2.26 us
where the time goes in v3:
time: 57.6 us; the launch traced here: 57.5 us
  Pallas kernels  54.6 us (95%)
  local copies, waits for them, and re-layouts  2.26 us (4%)
  between operations  0.64 us (1%)
    pallas_call x1, Pallas kernels, per_device(): pl.pallas_call(body, out_shape=(pltpu.VMEM((64, chans), BF16), pltpu.VMEM...  54.6 us
    unnamed x3, local copies, waits for them, and re-layouts  2.26 us

profile of v3, /device:TPU:56, one launch (start us, length us, event | category | flops | bytes accessed | tf_op | source)
XLA Modules:
  0.0 57.5 jit_solution(13859551175990228010)
XLA Ops:
  0.6 54.6 %shard_map.76 = (bf16[64,1024]{1,0:T(8,128)(2,1)S(1)}, bf16[1024,512]{1,0:T(8,128)(2,1)S(1)}, f32[32,512]{1,0:T(8,128)S(1)}) custom-call(s32[1,8]{1,0:T(1,128)} %refs_0_.1, s32[32]{0:T(128)} %refs_1_.1, bf16[8,128,512]{2,1,0:T(8,128)(2,1)} %bitcast.1, bf16[32,512]{1,0:T(8,128)(2,1)} %refs_3_.1, bf16[1024,1024]{1,0:T(8,128)(2,1)} %refs_4_.1), custom_call_target="tpu_custom_call" | custom-call | tf_op jit(solution)/shard_map/pallas_call | solution.py:416
  55.2 0.7 %copy.11 = bf16[64,1024]{1,0:T(8,128)(2,1)} copy(bf16[64,1024]{1,0:T(8,128)(2,1)S(1)} %get-tuple-element.3) | data formatting | bytes 262144
  55.9 0.6 %copy.13 = f32[32,512]{1,0:T(8,128)} copy(f32[32,512]{1,0:T(8,128)S(1)} %get-tuple-element.5) | data formatting | bytes 131072
  56.5 1.0 %copy.12 = bf16[1024,512]{1,0:T(8,128)(2,1)} copy(bf16[1024,512]{1,0:T(8,128)(2,1)S(1)} %get-tuple-element.4) | data formatting | bytes 2097152

commit v4 on v3

--- a/solution.py
+++ b/solution.py
@@ -401,6 +401,15 @@
         copy.wait_send()
 
 
+def write_out(kv, tg, wg, kv_out, tg_out, wg_out, sem):
+    pairs = [(tg, tg_out), (kv, kv_out), (wg, wg_out)]
+    copies = [pltpu.make_async_copy(a, o, sem.at[i]) for i, (a, o) in enumerate(pairs)]
+    for copy in copies:
+        copy.start()
+    for copy in copies:
+        copy.wait()
+
+
 def per_device(tokens, weight_t, cotangent, hard_ids, hard_count):
     factor = 1.0 / math.sqrt(lax.axis_size("dp") * HARD_DEV * L)
     rows, width = tokens.shape
@@ -413,7 +422,7 @@
     def body(*refs):
         kernel(factor, *refs)
 
-    return pl.pallas_call(
+    results = pl.pallas_call(
         body,
         out_shape=(
             pltpu.VMEM((64, chans), BF16),
@@ -460,6 +469,14 @@
         ],
         compiler_params=pltpu.CompilerParams(collective_id=0, has_side_effects=True),
     )(hard_ids, hard_count, tokens.reshape(SEQS, L, width), weight_t, cotangent)
+    results = [pltpu.with_memory_space_constraint(a, pltpu.VMEM) for a in results]
+    return pl.pallas_call(
+        write_out,
+        out_shape=tuple(jax.ShapeDtypeStruct(a.shape, a.dtype) for a in results),
+        in_specs=[vmem] * 3,
+        out_specs=(any_spec,) * 3,
+        scratch_shapes=[dma((3,))],
+    )(*results)
 
 
 def solution(mesh):

time: 57.6 us -> 56.4 us (0.979)
  local copies, waits for them, and re-layouts: 2.26 us -> 0 us
  Pallas kernels: 54.6 us -> 55.6 us
    unnamed x3 -> x0, local copies, waits for them, and re-layouts: 2.26 us -> none
    pallas_call x0 -> x1, Pallas kernels: none -> 1.05 us  [per_device(): pl.pallas_call(write_out, out_shape=tuple((jax.ShapeDtypeStruct(a.shape,...]
where the time goes in v4:
time: 56.4 us; the launch traced here: 56.3 us
  Pallas kernels  55.6 us (99%)
  between operations  0.64 us (1%)
    pallas_call x1, Pallas kernels, per_device(): pl.pallas_call(body, out_shape=(pltpu.VMEM((64, chans), BF16), pltpu.VMEM...  54.6 us

profile of v4, /device:TPU:56, one launch (start us, length us, event | category | flops | bytes accessed | tf_op | source)
XLA Modules:
  0.0 56.3 jit_solution(1745377154178430871)
XLA Ops:
  0.6 54.6 %shard_map.76 = (bf16[64,1024]{1,0:T(8,128)(2,1)S(1)}, bf16[1024,512]{1,0:T(8,128)(2,1)S(1)}, f32[32,512]{1,0:T(8,128)S(1)}) custom-call(s32[1,8]{1,0:T(1,128)} %refs_0_.1, s32[32]{0:T(128)} %refs_1_.1, bf16[8,128,512]{2,1,0:T(8,128)(2,1)} %bitcast.1, bf16[32,512]{1,0:T(8,128)(2,1)} %refs_3_.1, bf16[1024,1024]{1,0:T(8,128)(2,1)} %refs_4_.1), custom_call_target="tpu_custom_call" | custom-call | tf_op jit(solution)/shard_map/pallas_call | solution.py:425
  55.2 1.0 %shard_map.77 = (bf16[64,1024]{1,0:T(8,128)(2,1)}, bf16[1024,512]{1,0:T(8,128)(2,1)}, f32[32,512]{1,0:T(8,128)}) custom-call(bf16[64,1024]{1,0:T(8,128)(2,1)S(1)} %get-tuple-element.6.kv, bf16[1024,512]{1,0:T(8,128)(2,1)S(1)} %get-tuple-element.7.tg, f32[32,512]{1,0:T(8,128)S(1)} %get-tuple-element.8.wg), custom_call_target="tpu_custom_call" | custom-call | tf_op jit(solution)/shard_map/pallas_call | solution.py:473
